TPU v7x, 32 devices: a whole 2x2x4 slice. The times are simulated.
32 devices in a mesh: leaf: 32 (over z, y, x, core).
Axes of the slice: x: 2, y: 2, z: 4, core: 2. Of those that a mesh axis runs over, the one named last changes fastest.
Arguments:
- points: bfloat16 [64, 32768], P(None, 'leaf'), may hold values from -6 to 6
- weights: bfloat16 [32768, 512], P('leaf'), may hold values from -1.1953125 to 1.1953125
- interp: bfloat16 [32768, 512], P('leaf'), may hold values from -0.1875 to 0.1875
- transfers: bfloat16 [32, 5, 512, 512], P('leaf'), may hold values from -0.25 to 0.25
- near_mask: int32 [32, 4], P('leaf'), may hold values 0 or 1
- skel_index: int32 [32, 512], P('leaf'), may hold values from 0 to 1023, as said below
Outputs:
- product: bfloat16 [32768, 512], P('leaf')
Inputs may be any that keep to these rules, and one draw needn't show every extreme that they name: `skel_index`: each row holds 512 distinct ranks.
All inputs are finite; a program needn't handle non-finite values. No bound on the sum of `near_mask` on one device may be relied on, other than what follows from the above.
Results may differ from a plain program's by a relative error of at most 0.0075.
Values may be sent and summed in bfloat16 or wider, within the bound.
A program may use at most 128 MiB of HBM per device.

v0:
```python
import jax
import jax.numpy as jnp
from jax import lax
from jax.sharding import PartitionSpec as P


def passed_along(value, axis, steps):
    count = lax.axis_size(axis)
    leading, last = (max(0, -steps), min(count, count - steps))
    return lax.ppermute(value, axis, [(source, source + steps) for source in range(leading, last)])


def from_partner(value, axis, apart):
    mask = 2**apart
    pairs = [(source, source ^ mask) for source in range(lax.axis_size(axis))]
    return lax.ppermute(value, axis, pairs)


def kernel_tile(left, right):
    left_wide = left.astype(jnp.float32)
    right_wide = right.astype(jnp.float32)
    sq_left = jnp.sum(left_wide * left_wide, axis=0)
    sq_right = jnp.sum(right_wide * right_wide, axis=0)
    cross_terms = lax.dot_general(
        left, right, (((0,), (0,)), ((), ())), preferred_element_type=jnp.float32
    )
    distance = sq_left[:, None] + sq_right[None, :] - 2.0 * cross_terms
    return jnp.exp(distance * (-1.0 / left.shape[0])).astype(jnp.bfloat16)


def join_points(own_part, partner_part, upper_half):
    first_part = jnp.where(upper_half == 1, partner_part, own_part)
    second_part = jnp.where(upper_half == 1, own_part, partner_part)
    return jnp.concatenate([first_part, second_part], axis=1)


def coupled_block(own_nodes, sibling_nodes, sibling_sums):
    tile = kernel_tile(own_nodes.astype(jnp.bfloat16), sibling_nodes.astype(jnp.bfloat16))
    return jnp.dot(
        tile, sibling_sums.astype(jnp.bfloat16), preferred_element_type=jnp.float32
    ).astype(jnp.bfloat16)


def couple_level(own_nodes, sibling_nodes, sibling_sums, transfer):
    coupled = coupled_block(own_nodes, sibling_nodes, sibling_sums)
    return jnp.dot(transfer, coupled, preferred_element_type=jnp.float32)


def per_device(points, weights, interp, transfers, near_mask, skel_index):
    leaves = lax.axis_size("leaf")
    leaf_index = lax.axis_index("leaf")
    radius = near_mask.shape[1] // 2
    offsets = list(range(-radius, 0)) + list(range(1, radius + 1))
    near_field = jnp.dot(kernel_tile(points, points), weights, preferred_element_type=jnp.float32)
    blocks_by_offset = {}
    for direction in (1, -1):
        carried = (points, weights)
        for hop_count in range(radius):
            carried = passed_along((carried[0], carried[1]), "leaf", -direction)
            blocks_by_offset[direction * (hop_count + 1)] = carried
    for slot_index, offset in enumerate(offsets):
        other_points, other_weights = blocks_by_offset[offset]
        target = leaf_index + offset
        in_range = (target >= 0) & (target < leaves)
        flag_value = jnp.where(in_range, near_mask[0, slot_index], 0).astype(jnp.float32)
        block = jnp.dot(
            kernel_tile(points, other_points), other_weights, preferred_element_type=jnp.float32
        )
        near_field = near_field + flag_value * block
    width = skel_index.shape[1]
    levels = transfers.shape[1]
    skel_points = jnp.take(points, skel_index[0], axis=1).astype(jnp.float32)
    leaf_weights = lax.dot_general(
        interp, weights, (((0,), (0,)), ((), ())), preferred_element_type=jnp.float32
    ).astype(jnp.bfloat16)
    level_terms = jnp.einsum(
        "lab,ac->lbc", transfers[0], leaf_weights, preferred_element_type=jnp.float32
    )
    far_sum = jnp.zeros((width, weights.shape[1]), jnp.float32)
    for level in range(levels):
        node_sum = level_terms[level]
        node_cols = skel_points[:, : width >> level]
        for bit_level in range(level):
            upper_half = leaf_index >> bit_level & 1
            partner_sum, partner_cols = from_partner((node_sum, node_cols), "leaf", bit_level)
            node_sum = node_sum + partner_sum
            node_cols = join_points(node_cols, partner_cols, upper_half)
        sibling_sum, sibling_cols = (
            from_partner(node_sum.astype(jnp.bfloat16), "leaf", level).astype(node_sum.dtype),
            from_partner(node_cols.astype(jnp.bfloat16), "leaf", level).astype(node_cols.dtype),
        )
        far_sum = far_sum + couple_level(node_cols, sibling_cols, sibling_sum, transfers[0, level])
    far_skeleton = far_sum.astype(jnp.bfloat16)
    far_field = jnp.dot(interp, far_skeleton, preferred_element_type=jnp.float32)
    return (near_field + far_field).astype(jnp.bfloat16)


def solution(mesh):
    return jax.shard_map(
        per_device,
        mesh=mesh,
        in_specs=(
            P(None, "leaf"),
            P("leaf", None),
            P("leaf", None),
            P("leaf", None, None, None),
            P("leaf", None),
            P("leaf", None),
        ),
        out_specs=P("leaf", None),
        check_vma=False,
    )
```

profile of v0, /device:TPU:0, one launch (start us, length us, event | category | flops | bytes accessed | tf_op | source)
XLA Modules:
  0.0 254.6 jit_solution(216401023354210930)
XLA Ops:
  5.2 6.5 %fusion.2 = f32[5,512,512]{1,2,0:T(8,128)} fusion(bf16[1,5,512,512]{3,2,1,0:T(8,128)(2,1)} %param.9, bf16[1024,512]{1,0:T(8,128)(2,1)S(1)} %copy-done, bf16[1024,512]{1,0:T(8,128)(2,1)} %param.7), kind=kOutput, calls=%fused_computation.8 | convolution fusion | flops 1879310336 | bytes 9961472 | tf_op jit(solution)/shard_map/lab,ac->lbc/dot_general | solution.py:76
  11.7 4.4 %slice_bitcast_fusion = (f32[512,512]{0,1:T(8,128)}, f32[512,512]{0,1:T(8,128)}, f32[512,512]{0,1:T(8,128)}, f32[512,512]{0,1:T(8,128)}) fusion(f32[5,512,512]{1,2,0:T(8,128)} %fusion.2), kind=kLoop, calls=%fused_computation.34 | loop fusion | bytes 8388608 | tf_op jit(solution)/shard_map/squeeze | solution.py:81
  19.3 4.6 %fusion.10 = f32[1024,512]{1,0:T(8,128)} fusion(bf16[1024,512]{1,0:T(8,128)(2,1)} %param.7, bf16[64,1024]{1,0:T(8,128)(2,1)S(1)} %copy-done.4, f32[1024]{0:T(1024)S(1)} %multiply_reduce_fusion.14), kind=kOutput, calls=%fused_computation.30 | convolution fusion | flops 1213202432 | bytes 3280896 | tf_op jit(solution)/shard_map/dot_general | solution.py:54
  28.2 2.6 %collective-permute-start.29 = (bf16[64,64]{0,1:T(8,128)(2,1)S(1)}, bf16[64,64]{0,1:T(8,128)(2,1)S(1)}, u32[]{:S(2)}, u32[]{:S(2)}) collective-permute-start(bf16[64,64]{0,1:T(8,128)(2,1)S(1)} %pad_maximum_fusion.9), channel_id=1, source_target_pairs={{0,2},{1,3},{2,0},{3,1},{4,6},{5,7},{6,4},{7,5},{8,10},{9,11},{10,... | collective-permute-start | bytes 24584 | tf_op jit(solution)/shard_map/ppermute | solution.py:16
  70.4 5.4 %collective-permute-start.2 = (bf16[1024,512]{1,0:T(8,128)(2,1)}, bf16[1024,512]{1,0:T(8,128)(2,1)}, u32[]{:S(2)}, u32[]{:S(2)}) collective-permute-start(bf16[1024,512]{1,0:T(8,128)(2,1)} %param.7), channel_id=1, source_target_pairs={{0,1},{1,2},{2,3},{3,4},{4,5},{5,6},{6,7},{7,8},{8,9},{9,10},{10,1... | collective-permute-start | bytes 3145736 | tf_op jit(solution)/shard_map/ppermute | solution.py:10
  76.4 2.6 %collective-permute-start.32 = (bf16[64,512]{0,1:T(8,128)(2,1)S(1)}, bf16[64,512]{0,1:T(8,128)(2,1)S(1)}, u32[]{:S(2)}, u32[]{:S(2)}) collective-permute-start(bf16[64,512]{0,1:T(8,128)(2,1)S(1)} %pad_maximum_fusion.6), channel_id=1, source_target_pairs={{0,16},{1,17},{2,18},{3,19},{4,20},{5,21},{6,22},{7,23},{8,24},{9,... | collective-permute-start | bytes 196616 | tf_op jit(solution)/shard_map/ppermute | solution.py:16
  79.0 4.8 %fusion.79 = (f32[512,512]{0,1:T(8,128)S(1)}, f32[512,512]{0,1:T(8,128)S(1)}, f32[512,512]{0,1:T(8,128)}, bf16[512,512]{0,1:T(8,128)(2,1)}) fusion(f32[512,512]{0,1:T(8,128)S(1)} %collective-permute-done.33, f32[5,512,512]{1,2,0:T(8,128)} %fusion.2, f32[512,512]{0,1:T(8,128)} %collective-permute-done.24, f32[512,512]{0,1:T(8,128)} %collective-permute-done.17, ...), kind=kLoop, calls=%fused_computation.145 | loop fusion | flops 1310720 | bytes 12058624 | tf_op jit(solution)/shard_map/add | solution.py:86
  87.4 3.0 %collective-permute-start.1 = (bf16[64,1024]{1,0:T(8,128)(2,1)S(1)}, bf16[64,1024]{1,0:T(8,128)(2,1)S(1)}, u32[]{:S(2)}, u32[]{:S(2)}) collective-permute-start(bf16[64,1024]{1,0:T(8,128)(2,1)S(1)} %collective-permute-done), channel_id=1, source_target_pairs={{0,1},{1,2},{2,3},{3,4},{4,5},{5,6},{6,7},{7,8},{8,9},{9,10},{10,1... | collective-permute-start | bytes 393224 | tf_op jit(solution)/shard_map/ppermute | solution.py:10
  93.1 19.5 %collective-permute-start.9 = (bf16[512,512]{0,1:T(8,128)(2,1)S(1)}, bf16[512,512]{0,1:T(8,128)(2,1)S(1)}, u32[]{:S(2)}, u32[]{:S(2)}) collective-permute-start(bf16[512,512]{0,1:T(8,128)(2,1)S(1)} %copy-done.5), channel_id=1, source_target_pairs={{0,1},{1,0},{2,3},{3,2},{4,5},{5,4},{6,7},{7,6},{8,9},{9,8},{10,11... | collective-permute-start | bytes 1572872 | tf_op jit(solution)/shard_map/ppermute | solution.py:16
  118.0 24.2 %collective-permute-start.35 = (f32[512,512]{0,1:T(8,128)S(1)}, f32[512,512]{0,1:T(8,128)}, u32[]{:S(2)}, u32[]{:S(2)}) collective-permute-start(f32[512,512]{0,1:T(8,128)S(1)} %add.266), channel_id=1, source_target_pairs={{0,4},{1,5},{2,6},{3,7},{4,0},{5,1},{6,2},{7,3},{8,12},{9,13},{10,... | collective-permute-start | bytes 3145736 | tf_op jit(solution)/shard_map/ppermute | solution.py:16
  143.0 3.4 %fusion.8 = f32[512,512]{1,0:T(8,128)} fusion(bf16[512,512]{0,1:T(8,128)(2,1)} %copy-done.14, f32[512,512]{1,0:T(8,128)} %convolution_multiply_fusion.4, bf16[1,5,512,512]{3,2,1,0:T(8,128)(2,1)} %param.9, f32[512]{0:T(512)} %multiply_reduce_fusion.8, f32[512]{0:T(512)} %get-tuple-element.5), kind=kOutput, calls=%fused_computation.28 | convolution fusion | flops 538181632 | bytes 3149824 | tf_op jit(solution)/shard_map/dot_general | solution.py:46
  150.7 4.6 %fusion.12 = f32[1024,512]{1,0:T(8,128)} fusion(bf16[1024,512]{1,0:T(8,128)(2,1)} %collective-permute-done.2, bf16[64,1024]{1,0:T(8,128)(2,1)S(1)} %copy-done.4, bf16[64,1024]{1,0:T(8,128)(2,1)} %copy-done.7, f32[1024]{0:T(1024)} %multiply_reduce_fusion.12, f32[1024]{0:T(1024)S(1)} %multiply_reduce_fusion.14), kind=kOutput, calls=%fused_computation.32 | convolution fusion | flops 1213202432 | bytes 3416064 | tf_op jit(solution)/shard_map/dot_general | solution.py:66
  155.3 2.4 add.259
  157.7 3.5 %collective-permute-start.26 = (f32[512,512]{0,1:T(8,128)}, f32[512,512]{0,1:T(8,128)}, u32[]{:S(2)}, u32[]{:S(2)}) collective-permute-start(f32[512,512]{0,1:T(8,128)} %add.259), channel_id=1, source_target_pairs={{0,4},{1,5},{2,6},{3,7},{4,0},{5,1},{6,2},{7,3},{8,12},{9,13},{10,... | collective-permute-start | bytes 3145736 | tf_op jit(solution)/shard_map/ppermute | solution.py:16
  161.3 4.6 %fusion.13 = f32[1024,512]{1,0:T(8,128)} fusion(bf16[1024,512]{1,0:T(8,128)(2,1)} %collective-permute-done.5, bf16[64,1024]{1,0:T(8,128)(2,1)S(1)} %copy-done.4, bf16[64,1024]{1,0:T(8,128)(2,1)} %copy-done.10, f32[1024]{0:T(1024)S(1)} %multiply_reduce_fusion.11, f32[1024]{0:T(1024)S(1)} %multiply_reduce_fusion.14), kind=kOutput, calls=%fused_computation.33 | convolution fusion | flops 1213202432 | bytes 3416064 | tf_op jit(solution)/shard_map/dot_general | solution.py:66
  167.3 2.4 add.267
  169.7 2.7 %collective-permute-done.13 = bf16[512,512]{0,1:T(8,128)(2,1)} collective-permute-done((bf16[512,512]{0,1:T(8,128)(2,1)}, bf16[512,512]{0,1:T(8,128)(2,1)}, u32[]{:S(2)}, u32[]{:S(2)}) %collective-permute-start.13) | collective-permute-done | bytes 524320 | tf_op jit(solution)/shard_map/ppermute | solution.py:16
  172.4 10.4 %collective-permute-start.36 = (f32[512,512]{0,1:T(8,128)}, f32[512,512]{0,1:T(8,128)}, u32[]{:S(2)}, u32[]{:S(2)}) collective-permute-start(f32[512,512]{0,1:T(8,128)} %add.267), channel_id=1, source_target_pairs={{0,8},{1,9},{2,10},{3,11},{4,12},{5,13},{6,14},{7,15},{8,0},{9,1},... | collective-permute-start | bytes 3145736 | tf_op jit(solution)/shard_map/ppermute | solution.py:16
  182.8 3.8 %convolution_add_fusion.3 = f32[512,512]{1,0:T(8,128)} fusion(f32[512,512]{1,0:T(8,128)} %fusion.8, bf16[512,512]{0,1:T(8,128)(2,1)} %collective-permute-done.13, f32[512,512]{1,0:T(8,128)} %convolution_multiply_fusion.3, bf16[1,5,512,512]{3,2,1,0:T(8,128)(2,1)} %param.9, f32[512]{0:T(512)} %multiply_reduce_fusion.6, f32[512]{0:T(512)} %multiply_reduce_fusion.7), kind=kOutput, calls=%fused_computation.17 | convolution fusion | flops 538443776 | bytes 4198400 | tf_op jit(solution)/shard_map/dot_general | solution.py:46
  186.6 8.3 %collective-permute-done.18 = f32[512,512]{0,1:T(8,128)} collective-permute-done((f32[512,512]{0,1:T(8,128)}, f32[512,512]{0,1:T(8,128)}, u32[]{:S(2)}, u32[]{:S(2)}) %collective-permute-start.18) | collective-permute-done | bytes 1048608 | tf_op jit(solution)/shard_map/ppermute | solution.py:16
  197.2 4.6 %fusion.11 = f32[1024,512]{1,0:T(8,128)} fusion(bf16[1024,512]{1,0:T(8,128)(2,1)} %collective-permute-done.3, bf16[64,1024]{1,0:T(8,128)(2,1)S(1)} %copy-done.4, bf16[64,1024]{1,0:T(8,128)(2,1)S(1)} %copy-done.9, f32[1024]{0:T(1024)S(1)} %multiply_reduce_fusion.13, f32[1024]{0:T(1024)S(1)} %multiply_reduce_fusion.14), kind=kOutput, calls=%fused_computation.31 | convolution fusion | flops 1213202432 | bytes 3416064 | tf_op jit(solution)/shard_map/dot_general | solution.py:66
  201.8 2.6 %add_convert_fusion.1 = bf16[512,512]{0,1:T(8,128)(2,1)} fusion(f32[512,512]{0,1:T(8,128)} %add.259, f32[512,512]{0,1:T(8,128)} %collective-permute-done.26), kind=kLoop, calls=%fused_computation.41 | loop fusion | flops 524288 | bytes 2621440 | tf_op jit(solution)/shard_map/convert_element_type | solution.py:89
  204.4 9.8 %collective-permute-start.27 = (bf16[512,512]{0,1:T(8,128)(2,1)}, bf16[512,512]{0,1:T(8,128)(2,1)}, u32[]{:S(2)}, u32[]{:S(2)}) collective-permute-start(bf16[512,512]{0,1:T(8,128)(2,1)} %add_convert_fusion.1), channel_id=1, source_target_pairs={{0,8},{1,9},{2,10},{3,11},{4,12},{5,13},{6,14},{7,15},{8,0},{9,1},... | collective-permute-start | bytes 1572872 | tf_op jit(solution)/shard_map/ppermute | solution.py:16
  214.2 2.9 %collective-permute-done.36 = f32[512,512]{0,1:T(8,128)} collective-permute-done((f32[512,512]{0,1:T(8,128)}, f32[512,512]{0,1:T(8,128)}, u32[]{:S(2)}, u32[]{:S(2)}) %collective-permute-start.36) | collective-permute-done | bytes 1048608 | tf_op jit(solution)/shard_map/ppermute | solution.py:16
  217.1 2.5 add_convert_fusion
  221.7 3.4 %convolution_add_fusion.2 = f32[512,512]{1,0:T(8,128)} fusion(f32[512,512]{1,0:T(8,128)} %convolution_add_fusion.3, bf16[512,512]{0,1:T(8,128)(2,1)} %collective-permute-done.19, f32[512,512]{1,0:T(8,128)S(1)} %copy-done.2, bf16[1,5,512,512]{3,2,1,0:T(8,128)(2,1)} %param.9, f32[512]{0:T(512)} %multiply_reduce_fusion.4, f32[512]{0:T(512)S(1)} %copy-done.12), kind=kOutput, calls=%fused_computation.15 | convolution fusion | flops 538443776 | bytes 4198400 | tf_op jit(solution)/shard_map/dot_general | solution.py:46
  225.2 11.0 %collective-permute-done.27 = bf16[512,512]{0,1:T(8,128)(2,1)} collective-permute-done((bf16[512,512]{0,1:T(8,128)(2,1)}, bf16[512,512]{0,1:T(8,128)(2,1)}, u32[]{:S(2)}, u32[]{:S(2)}) %collective-permute-start.27) | collective-permute-done | bytes 524320 | tf_op jit(solution)/shard_map/ppermute | solution.py:16
  236.2 3.4 %convolution_add_fusion.1 = f32[512,512]{1,0:T(8,128)} fusion(f32[512,512]{1,0:T(8,128)} %convolution_add_fusion.2, bf16[512,512]{0,1:T(8,128)(2,1)} %collective-permute-done.27, f32[512,512]{1,0:T(8,128)S(1)} %copy-done.3, bf16[1,5,512,512]{3,2,1,0:T(8,128)(2,1)} %param.9, f32[512]{0:T(512)} %multiply_reduce_fusion.2, f32[512]{0:T(512)S(1)} %copy-done.13), kind=kOutput, calls=%fused_computation.13 | convolution fusion | flops 538443776 | bytes 4198400 | tf_op jit(solution)/shard_map/dot_general | solution.py:46
  239.6 2.6 %collective-permute-done.37 = bf16[512,512]{0,1:T(8,128)(2,1)} collective-permute-done((bf16[512,512]{0,1:T(8,128)(2,1)}, bf16[512,512]{0,1:T(8,128)(2,1)}, u32[]{:S(2)}, u32[]{:S(2)}) %collective-permute-start.37) | collective-permute-done | bytes 524320 | tf_op jit(solution)/shard_map/ppermute | solution.py:16
  242.3 2.6 %convolution_convert_fusion = bf16[512,512]{1,0:T(8,128)(2,1)} fusion(bf16[512,512]{0,1:T(8,128)(2,1)} %collective-permute-done.37, bf16[64,512]{0,1:T(8,128)(2,1)S(1)} %collective-permute-done.32, f32[512]{0:T(512)} %multiply_reduce_fusion, f32[512]{0:T(512)} %multiply_reduce_fusion.1, bf16[64,256]{0,1:T(8,128)(2,1)S(1)} %get-tuple-element.24, ...), kind=kOutput, calls=%fused_computation.20 | convolution fusion | flops 303693824 | bytes 1183744 | tf_op jit(solution)/shard_map/dot_general | solution.py:39
  244.8 2.7 %fusion.9 = f32[512,1024]{0,1:T(8,128)S(1)} fusion(bf16[1024,512]{1,0:T(8,128)(2,1)S(1)} %copy-done, f32[512,512]{1,0:T(8,128)} %convolution_add_fusion.1, bf16[512,512]{1,0:T(8,128)(2,1)} %convolution_convert_fusion, bf16[1,5,512,512]{3,2,1,0:T(8,128)(2,1)} %param.9), kind=kOutput, calls=%fused_computation.29 | convolution fusion | flops 805830656 | bytes 5242880 | tf_op jit(solution)/shard_map/dot_general | solution.py:94
  247.5 7.1 %fusion.5 = bf16[1024,512]{1,0:T(8,128)(2,1)} fusion(f32[512,1024]{0,1:T(8,128)S(1)} %fusion.9, f32[1024,512]{1,0:T(8,128)} %fusion.13, f32[1024,512]{1,0:T(8,128)} %fusion.12, f32[1024,512]{1,0:T(8,128)} %fusion.10, f32[1024,512]{1,0:T(8,128)} %fusion.11, bf16[1024,512]{1,0:T(8,128)(2,1)} %collective-permute-done.7, bf16[64,1024]{1,0:T(8,128)(2,1)S(1)} %copy-done.4, ...), kind=kOutput, calls=%fused_computation.10 | convolution fusion | flops 1218445312 | bytes 12853264 | tf_op jit(solution)/shard_map/dot_general | solution.py:66
  (144 shorter events, 72.7 us)
Async XLA Ops:
  4.7 51.9 %collective-permute-start.8 = (bf16[64,512]{0,1:T(8,128)(2,1)S(1)}, bf16[64,512]{0,1:T(8,128)(2,1)S(1)}, u32[]{:S(2)}, u32[]{:S(2)}) collective-permute-start(bf16[64,512]{0,1:T(8,128)(2,1)S(1)} %get-tuple-element.6), channel_id=1, source_target_pairs={{0,1},{1,0},{2,3},{3,2},{4,5},{5,4},{6,7},{7,6},{8,9},{9,8},{10,11... | collective-permute-start | bytes 196616 | tf_op jit(solution)/shard_map/ppermute | solution.py:16
  5.2 21.7 %collective-permute-start.28 = (bf16[64,32]{0,1:T(8,128)(2,1)S(1)}, bf16[64,32]{0,1:T(8,128)(2,1)S(1)}, u32[]{:S(2)}, u32[]{:S(2)}) collective-permute-start(bf16[64,32]{0,1:T(8,128)(2,1)S(1)} %slice.82), channel_id=1, source_target_pairs={{0,1},{1,0},{2,3},{3,2},{4,5},{5,4},{6,7},{7,6},{8,9},{9,8},{10,11... | collective-permute-start | bytes 12296 | tf_op jit(solution)/shard_map/ppermute | solution.py:16
  16.1 54.2 %collective-permute-start.12 = (f32[512,512]{0,1:T(8,128)}, f32[512,512]{0,1:T(8,128)S(1)}, u32[]{:S(2)}, u32[]{:S(2)}) collective-permute-start(f32[512,512]{0,1:T(8,128)} %get-tuple-element.14), channel_id=1, source_target_pairs={{0,1},{1,0},{2,3},{3,2},{4,5},{5,4},{6,7},{7,6},{8,9},{9,8},{10,11... | collective-permute-start | bytes 3145736 | tf_op jit(solution)/shard_map/ppermute | solution.py:16
  16.6 59.2 %collective-permute-start.17 = (f32[512,512]{0,1:T(8,128)}, f32[512,512]{0,1:T(8,128)}, u32[]{:S(2)}, u32[]{:S(2)}) collective-permute-start(f32[512,512]{0,1:T(8,128)} %get-tuple-element.13), channel_id=1, source_target_pairs={{0,1},{1,0},{2,3},{3,2},{4,5},{5,4},{6,7},{7,6},{8,9},{9,8},{10,11... | collective-permute-start | bytes 3145736 | tf_op jit(solution)/shard_map/ppermute | solution.py:16
  16.6 59.8 %collective-permute-start.24 = (f32[512,512]{0,1:T(8,128)}, f32[512,512]{0,1:T(8,128)}, u32[]{:S(2)}, u32[]{:S(2)}) collective-permute-start(f32[512,512]{0,1:T(8,128)} %get-tuple-element.12), channel_id=1, source_target_pairs={{0,1},{1,0},{2,3},{3,2},{4,5},{5,4},{6,7},{7,6},{8,9},{9,8},{10,11... | collective-permute-start | bytes 3145736 | tf_op jit(solution)/shard_map/ppermute | solution.py:16
  28.2 4.4 %collective-permute-start.29 = (bf16[64,64]{0,1:T(8,128)(2,1)S(1)}, bf16[64,64]{0,1:T(8,128)(2,1)S(1)}, u32[]{:S(2)}, u32[]{:S(2)}) collective-permute-start(bf16[64,64]{0,1:T(8,128)(2,1)S(1)} %pad_maximum_fusion.9), channel_id=1, source_target_pairs={{0,2},{1,3},{2,0},{3,1},{4,6},{5,7},{6,4},{7,5},{8,10},{9,11},{10,... | collective-permute-start | bytes 24584 | tf_op jit(solution)/shard_map/ppermute | solution.py:16
  42.8 4.4 %collective-permute-start.15 = (bf16[64,256]{0,1:T(8,128)(2,1)S(1)}, bf16[64,256]{0,1:T(8,128)(2,1)S(1)}, u32[]{:S(2)}, u32[]{:S(2)}) collective-permute-start(bf16[64,256]{0,1:T(8,128)(2,1)S(1)} %pad_maximum_fusion.1), channel_id=1, source_target_pairs={{0,2},{1,3},{2,0},{3,1},{4,6},{5,7},{6,4},{7,5},{8,10},{9,11},{10,... | collective-permute-start | bytes 98312 | tf_op jit(solution)/shard_map/ppermute | solution.py:16
  47.2 4.3 %collective-permute-start.22 = (bf16[64,256]{0,1:T(8,128)(2,1)S(1)}, bf16[64,256]{0,1:T(8,128)(2,1)S(1)}, u32[]{:S(2)}, u32[]{:S(2)}) collective-permute-start(bf16[64,256]{0,1:T(8,128)(2,1)S(1)} %pad_maximum_fusion.3), channel_id=1, source_target_pairs={{0,4},{1,5},{2,6},{3,7},{4,0},{5,1},{6,2},{7,3},{8,12},{9,13},{10,... | collective-permute-start | bytes 98312 | tf_op jit(solution)/shard_map/ppermute | solution.py:16
  51.5 4.3 %collective-permute-start.31 = (bf16[64,256]{0,1:T(8,128)(2,1)S(1)}, bf16[64,256]{0,1:T(8,128)(2,1)S(1)}, u32[]{:S(2)}, u32[]{:S(2)}) collective-permute-start(bf16[64,256]{0,1:T(8,128)(2,1)S(1)} %pad_maximum_fusion.5), channel_id=1, source_target_pairs={{0,8},{1,9},{2,10},{3,11},{4,12},{5,13},{6,14},{7,15},{8,0},{9,1},... | collective-permute-start | bytes 98312 | tf_op jit(solution)/shard_map/ppermute | solution.py:16
  55.8 23.2 %collective-permute-start.33 = (f32[512,512]{0,1:T(8,128)}, f32[512,512]{0,1:T(8,128)S(1)}, u32[]{:S(2)}, u32[]{:S(2)}) collective-permute-start(f32[512,512]{0,1:T(8,128)} %get-tuple-element.11), channel_id=1, source_target_pairs={{0,1},{1,0},{2,3},{3,2},{4,5},{5,4},{6,7},{7,6},{8,9},{9,8},{10,11... | collective-permute-start | bytes 3145736 | tf_op jit(solution)/shard_map/ppermute | solution.py:16
  56.6 6.0 %collective-permute-start.11 = (bf16[64,512]{0,1:T(8,128)(2,1)S(1)}, bf16[64,512]{0,1:T(8,128)(2,1)S(1)}, u32[]{:S(2)}, u32[]{:S(2)}) collective-permute-start(bf16[64,512]{0,1:T(8,128)(2,1)S(1)} %pad_maximum_fusion), channel_id=1, source_target_pairs={{0,2},{1,3},{2,0},{3,1},{4,6},{5,7},{6,4},{7,5},{8,10},{9,11},{10,... | collective-permute-start | bytes 196616 | tf_op jit(solution)/shard_map/ppermute | solution.py:16
  62.6 5.2 %collective-permute-start.16 = (bf16[64,512]{0,1:T(8,128)(2,1)S(1)}, bf16[64,512]{0,1:T(8,128)(2,1)S(1)}, u32[]{:S(2)}, u32[]{:S(2)}) collective-permute-start(bf16[64,512]{0,1:T(8,128)(2,1)S(1)} %pad_maximum_fusion.2), channel_id=1, source_target_pairs={{0,4},{1,5},{2,6},{3,7},{4,0},{5,1},{6,2},{7,3},{8,12},{9,13},{10,... | collective-permute-start | bytes 196616 | tf_op jit(solution)/shard_map/ppermute | solution.py:16
  67.8 19.6 %collective-permute-start = (bf16[64,1024]{1,0:T(8,128)(2,1)S(1)}, bf16[64,1024]{1,0:T(8,128)(2,1)S(1)}, u32[]{:S(2)}, u32[]{:S(2)}) collective-permute-start(bf16[64,1024]{1,0:T(8,128)(2,1)S(1)} %copy-done.4), channel_id=1, source_target_pairs={{0,1},{1,2},{2,3},{3,4},{4,5},{5,6},{6,7},{7,8},{8,9},{9,10},{10,1... | collective-permute-start | bytes 393224 | tf_op jit(solution)/shard_map/ppermute | solution.py:10
  70.4 76.0 %collective-permute-start.2 = (bf16[1024,512]{1,0:T(8,128)(2,1)}, bf16[1024,512]{1,0:T(8,128)(2,1)}, u32[]{:S(2)}, u32[]{:S(2)}) collective-permute-start(bf16[1024,512]{1,0:T(8,128)(2,1)} %param.7), channel_id=1, source_target_pairs={{0,1},{1,2},{2,3},{3,4},{4,5},{5,6},{6,7},{7,8},{8,9},{9,10},{10,1... | collective-permute-start | bytes 3145736 | tf_op jit(solution)/shard_map/ppermute | solution.py:10
  75.8 10.3 %collective-permute-start.23 = (bf16[64,512]{0,1:T(8,128)(2,1)S(1)}, bf16[64,512]{0,1:T(8,128)(2,1)S(1)}, u32[]{:S(2)}, u32[]{:S(2)}) collective-permute-start(bf16[64,512]{0,1:T(8,128)(2,1)S(1)} %pad_maximum_fusion.4), channel_id=1, source_target_pairs={{0,8},{1,9},{2,10},{3,11},{4,12},{5,13},{6,14},{7,15},{8,0},{9,1},... | collective-permute-start | bytes 196616 | tf_op jit(solution)/shard_map/ppermute | solution.py:16
  76.4 14.0 %collective-permute-start.32 = (bf16[64,512]{0,1:T(8,128)(2,1)S(1)}, bf16[64,512]{0,1:T(8,128)(2,1)S(1)}, u32[]{:S(2)}, u32[]{:S(2)}) collective-permute-start(bf16[64,512]{0,1:T(8,128)(2,1)S(1)} %pad_maximum_fusion.6), channel_id=1, source_target_pairs={{0,16},{1,17},{2,18},{3,19},{4,20},{5,21},{6,22},{7,23},{8,24},{9,... | collective-permute-start | bytes 196616 | tf_op jit(solution)/shard_map/ppermute | solution.py:16
  83.8 33.9 %collective-permute-start.34 = (f32[512,512]{0,1:T(8,128)S(1)}, f32[512,512]{0,1:T(8,128)S(1)}, u32[]{:S(2)}, u32[]{:S(2)}) collective-permute-start(f32[512,512]{0,1:T(8,128)S(1)} %get-tuple-element.7), channel_id=1, source_target_pairs={{0,2},{1,3},{2,0},{3,1},{4,6},{5,7},{6,4},{7,5},{8,10},{9,11},{10,... | collective-permute-start | bytes 3145736 | tf_op jit(solution)/shard_map/ppermute | solution.py:16
  86.1 7.0 %collective-permute-start.4 = (bf16[64,1024]{1,0:T(8,128)(2,1)S(1)}, bf16[64,1024]{1,0:T(8,128)(2,1)S(1)}, u32[]{:S(2)}, u32[]{:S(2)}) collective-permute-start(bf16[64,1024]{1,0:T(8,128)(2,1)S(1)} %copy-done.4), channel_id=1, source_target_pairs={{1,0},{2,1},{3,2},{4,3},{5,4},{6,5},{7,6},{8,7},{9,8},{10,9},{11,1... | collective-permute-start | bytes 393224 | tf_op jit(solution)/shard_map/ppermute | solution.py:10
  87.4 25.1 %collective-permute-start.1 = (bf16[64,1024]{1,0:T(8,128)(2,1)S(1)}, bf16[64,1024]{1,0:T(8,128)(2,1)S(1)}, u32[]{:S(2)}, u32[]{:S(2)}) collective-permute-start(bf16[64,1024]{1,0:T(8,128)(2,1)S(1)} %collective-permute-done), channel_id=1, source_target_pairs={{0,1},{1,2},{2,3},{3,4},{4,5},{5,6},{6,7},{7,8},{8,9},{9,10},{10,1... | collective-permute-start | bytes 393224 | tf_op jit(solution)/shard_map/ppermute | solution.py:10
  90.4 58.0 %collective-permute-start.25 = (f32[512,512]{0,1:T(8,128)S(1)}, f32[512,512]{0,1:T(8,128)}, u32[]{:S(2)}, u32[]{:S(2)}) collective-permute-start(f32[512,512]{0,1:T(8,128)S(1)} %get-tuple-element.8), channel_id=1, source_target_pairs={{0,2},{1,3},{2,0},{3,1},{4,6},{5,7},{6,4},{7,5},{8,10},{9,11},{10,... | collective-permute-start | bytes 3145736 | tf_op jit(solution)/shard_map/ppermute | solution.py:16
  93.1 49.1 %collective-permute-start.9 = (bf16[512,512]{0,1:T(8,128)(2,1)S(1)}, bf16[512,512]{0,1:T(8,128)(2,1)S(1)}, u32[]{:S(2)}, u32[]{:S(2)}) collective-permute-start(bf16[512,512]{0,1:T(8,128)(2,1)S(1)} %copy-done.5), channel_id=1, source_target_pairs={{0,1},{1,0},{2,3},{3,2},{4,5},{5,4},{6,7},{7,6},{8,9},{9,8},{10,11... | collective-permute-start | bytes 1572872 | tf_op jit(solution)/shard_map/ppermute | solution.py:16
  116.3 41.4 %collective-permute-start.5 = (bf16[1024,512]{1,0:T(8,128)(2,1)}, bf16[1024,512]{1,0:T(8,128)(2,1)}, u32[]{:S(2)}, u32[]{:S(2)}) collective-permute-start(bf16[1024,512]{1,0:T(8,128)(2,1)} %param.7), channel_id=1, source_target_pairs={{1,0},{2,1},{3,2},{4,3},{5,4},{6,5},{7,6},{8,7},{9,8},{10,9},{11,1... | collective-permute-start | bytes 3145736 | tf_op jit(solution)/shard_map/ppermute | solution.py:10
  118.0 47.9 %collective-permute-start.35 = (f32[512,512]{0,1:T(8,128)S(1)}, f32[512,512]{0,1:T(8,128)}, u32[]{:S(2)}, u32[]{:S(2)}) collective-permute-start(f32[512,512]{0,1:T(8,128)S(1)} %add.266), channel_id=1, source_target_pairs={{0,4},{1,5},{2,6},{3,7},{4,0},{5,1},{6,2},{7,3},{8,12},{9,13},{10,... | collective-permute-start | bytes 3145736 | tf_op jit(solution)/shard_map/ppermute | solution.py:16
  146.4 26.1 %collective-permute-start.13 = (bf16[512,512]{0,1:T(8,128)(2,1)}, bf16[512,512]{0,1:T(8,128)(2,1)}, u32[]{:S(2)}, u32[]{:S(2)}) collective-permute-start(bf16[512,512]{0,1:T(8,128)(2,1)} %get-tuple-element.10), channel_id=1, source_target_pairs={{0,2},{1,3},{2,0},{3,1},{4,6},{5,7},{6,4},{7,5},{8,10},{9,11},{10,... | collective-permute-start | bytes 1572872 | tf_op jit(solution)/shard_map/ppermute | solution.py:16
  146.4 48.5 %collective-permute-start.18 = (f32[512,512]{0,1:T(8,128)}, f32[512,512]{0,1:T(8,128)}, u32[]{:S(2)}, u32[]{:S(2)}) collective-permute-start(f32[512,512]{0,1:T(8,128)} %get-tuple-element.9), channel_id=1, source_target_pairs={{0,2},{1,3},{2,0},{3,1},{4,6},{5,7},{6,4},{7,5},{8,10},{9,11},{10,... | collective-permute-start | bytes 3145736 | tf_op jit(solution)/shard_map/ppermute | solution.py:16
  148.4 48.8 %collective-permute-start.3 = (bf16[1024,512]{1,0:T(8,128)(2,1)}, bf16[1024,512]{1,0:T(8,128)(2,1)}, u32[]{:S(2)}, u32[]{:S(2)}) collective-permute-start(bf16[1024,512]{1,0:T(8,128)(2,1)} %collective-permute-done.2), channel_id=1, source_target_pairs={{0,1},{1,2},{2,3},{3,4},{4,5},{5,6},{6,7},{7,8},{8,9},{9,10},{10,1... | collective-permute-start | bytes 3145736 | tf_op jit(solution)/shard_map/ppermute | solution.py:10
  157.7 44.1 %collective-permute-start.26 = (f32[512,512]{0,1:T(8,128)}, f32[512,512]{0,1:T(8,128)}, u32[]{:S(2)}, u32[]{:S(2)}) collective-permute-start(f32[512,512]{0,1:T(8,128)} %add.259), channel_id=1, source_target_pairs={{0,4},{1,5},{2,6},{3,7},{4,0},{5,1},{6,2},{7,3},{8,12},{9,13},{10,... | collective-permute-start | bytes 3145736 | tf_op jit(solution)/shard_map/ppermute | solution.py:16
  165.9 81.6 %collective-permute-start.7 = (bf16[1024,512]{1,0:T(8,128)(2,1)}, bf16[1024,512]{1,0:T(8,128)(2,1)}, u32[]{:S(2)}, u32[]{:S(2)}) collective-permute-start(bf16[1024,512]{1,0:T(8,128)(2,1)} %collective-permute-done.5), channel_id=1, source_target_pairs={{1,0},{2,1},{3,2},{4,3},{5,4},{6,5},{7,6},{8,7},{9,8},{10,9},{11,1... | collective-permute-start | bytes 3145736 | tf_op jit(solution)/shard_map/ppermute | solution.py:10
  172.4 44.6 %collective-permute-start.36 = (f32[512,512]{0,1:T(8,128)}, f32[512,512]{0,1:T(8,128)}, u32[]{:S(2)}, u32[]{:S(2)}) collective-permute-start(f32[512,512]{0,1:T(8,128)} %add.267), channel_id=1, source_target_pairs={{0,8},{1,9},{2,10},{3,11},{4,12},{5,13},{6,14},{7,15},{8,0},{9,1},... | collective-permute-start | bytes 3145736 | tf_op jit(solution)/shard_map/ppermute | solution.py:16
  197.1 24.6 %collective-permute-start.19 = (bf16[512,512]{0,1:T(8,128)(2,1)}, bf16[512,512]{0,1:T(8,128)(2,1)}, u32[]{:S(2)}, u32[]{:S(2)}) collective-permute-start(bf16[512,512]{0,1:T(8,128)(2,1)} %add_convert_fusion.2), channel_id=1, source_target_pairs={{0,4},{1,5},{2,6},{3,7},{4,0},{5,1},{6,2},{7,3},{8,12},{9,13},{10,... | collective-permute-start | bytes 1572872 | tf_op jit(solution)/shard_map/ppermute | solution.py:16
  204.4 31.8 %collective-permute-start.27 = (bf16[512,512]{0,1:T(8,128)(2,1)}, bf16[512,512]{0,1:T(8,128)(2,1)}, u32[]{:S(2)}, u32[]{:S(2)}) collective-permute-start(bf16[512,512]{0,1:T(8,128)(2,1)} %add_convert_fusion.1), channel_id=1, source_target_pairs={{0,8},{1,9},{2,10},{3,11},{4,12},{5,13},{6,14},{7,15},{8,0},{9,1},... | collective-permute-start | bytes 1572872 | tf_op jit(solution)/shard_map/ppermute | solution.py:16
  219.5 22.7 %collective-permute-start.37 = (bf16[512,512]{0,1:T(8,128)(2,1)}, bf16[512,512]{0,1:T(8,128)(2,1)}, u32[]{:S(2)}, u32[]{:S(2)}) collective-permute-start(bf16[512,512]{0,1:T(8,128)(2,1)} %add_convert_fusion), channel_id=1, source_target_pairs={{0,16},{1,17},{2,18},{3,19},{4,20},{5,21},{6,22},{7,23},{8,24},{9,... | collective-permute-start | bytes 1572872 | tf_op jit(solution)/shard_map/ppermute | solution.py:16
  (21 other events, 326.7 us)
where the time goes:
time: 256 us; the launch traced here: 255 us
  starting transfers between devices  112 us (44%)
  matrix products  56.5 us (22%)
  waiting for transfers between devices  45.8 us (18%)
  other arithmetic  27.1 us (11%)
  local copies, waits for them, and re-layouts  10.4 us (4%)
  between operations  2.78 us (1%)
    ppermute x30, starting transfers between devices, from_partner(): return lax.ppermute(value, axis, pairs)  94.6 us
    ppermute x30, waiting for transfers between devices, from_partner(): return lax.ppermute(value, axis, pairs)  44.7 us
    dot_general x4, matrix products, per_device(): jnp.dot(kernel_tile(points, other_points), other_weights, preferred_eleme...  21 us
    ppermute x8, starting transfers between devices, passed_along(): lax.ppermute(value, axis, [(source, source + steps) for source in range(l...  17.3 us
    dot_general x4, matrix products, couple_level(): return jnp.dot(transfer, coupled, preferred_element_type=jnp.float32)  14 us
    add x4, other arithmetic, per_device(): node_sum = node_sum + partner_sum  9.88 us
    convert_element_type x3, other arithmetic, per_device(): node_sum.astype(jnp.bfloat16)  7.24 us
    dot_general x1, matrix products, per_device(): jnp.einsum('lab,ac->lbc', transfers[0], leaf_weights, preferred_element_t...  6.51 us
  transfers between devices with their start and end apart: 38, of which 17 were waited for; matrix products, arithmetic and copies ran while one was open for 32% of the time, Pallas kernels for 0%

commit v1 on v0

v1 whole, which is shorter than its diff:
```python
import functools
import math

import jax
import jax.numpy as jnp
from jax import lax
from jax.experimental import pallas as pl
from jax.experimental.pallas import tpu as pltpu
from jax.sharding import PartitionSpec as P

MESH = pl.DeviceIdType.MESH
LANES = 128
CHUNKS = 4
F32, BF16 = jnp.float32, jnp.bfloat16


def rounded(value):
    return value.astype(BF16).astype(F32)


def dot(left, right, dims=((1,), (0,))):
    return lax.dot_general(left, right, (dims, ((), ())), preferred_element_type=F32)


def left_form(wide, dim):
    lane = lax.broadcasted_iota(jnp.int32, wide.shape, 1)
    norm = jnp.sum(jnp.where((lane >= dim) & (lane < dim + 3), wide, 0.0), axis=1, keepdims=True)
    left = jnp.where(lane < dim, 2.0 * wide, jnp.where(lane < dim + 3, -1.0, 0.0))
    return left.astype(BF16), norm


def reduce_bits(level):
    return [0] + list(range(level - 1, 0, -1)) if level else []


def plan(levels):
    names = []
    for level in range(levels):
        for bit in reduce_bits(level):
            names += [("rs", level, bit), ("ag", level, bit)]
        names += [("ex", level), ("pt", level)]
    for chunk in range(CHUNKS + 1):
        names += [("own_mate", chunk), ("own_x", chunk), ("fwd", chunk), ("fwd_mate", chunk)]
    return {name: at for at, name in enumerate(names)}


def body(
    count, slots,
    pts, w, interp, trans, mask, index,
    out,
    rown, lown, nown, rbuf, wbuf, near, lw, keep, tx, rx, sib, pbuf, psib, far,
    send_sem, recv_sem,
):
    me = lax.axis_index("leaf")
    core, chip = lax.rem(me, 2), lax.rem(me // 2, 2)
    dim, npts = pts.shape
    rank, rhs = lw.shape
    levels = trans.shape[0]
    deep = rown.shape[0]
    scale = math.log2(math.e) / dim

    def partner(bit):
        on = lax.rem(me // (1 << bit), 2)
        return me + (1 - 2 * on) * (1 << bit), on

    mate, xmate = partner(0)[0], partner(1)[0]
    ahead = me + 4 * (1 - 2 * chip)
    behind = me - 4 * (1 - 2 * chip)
    has_ahead = (ahead >= 0) & (ahead < count)
    has_behind = (behind >= 0) & (behind < count)

    def copy(name, src, dst, device):
        at = slots[name]
        return pltpu.make_async_remote_copy(
            src_ref=src, dst_ref=dst, send_sem=send_sem.at[at], recv_sem=recv_sem.at[at],
            device_id=(device,), device_id_type=MESH,
        )

    barrier = pltpu.get_barrier_semaphore()
    for bit in range(levels):
        pl.semaphore_signal(barrier, inc=1, device_id=(partner(bit)[0],), device_id_type=MESH)
    for other, there in ((ahead, has_ahead), (behind, has_behind)):
        @pl.when(there)
        def _():
            pl.semaphore_signal(barrier, inc=1, device_id=(other,), device_id_type=MESH)

    wide = pts[...].astype(F32)
    norm = jnp.sum(wide * wide, axis=0, keepdims=True)
    high = rounded(norm)
    middle = rounded(norm - high)
    low = norm - high - middle
    row = lax.broadcasted_iota(jnp.int32, (LANES - dim, npts), 0)
    extra = jnp.where(row == 0, high, jnp.where(row == 1, middle, jnp.where(row == 2, low, 0.0)))
    full = jnp.concatenate([wide, extra], axis=0)
    rown[...] = full[:deep].astype(BF16)
    left, norm_column = left_form(jnp.transpose(full), dim)
    lown[...] = left
    nown[...] = norm_column
    chosen = (lax.broadcasted_iota(jnp.int32, (npts, rank), 0) == index[...]).astype(BF16)
    pbuf[0] = jnp.transpose(dot(full.astype(BF16), chosen)).astype(BF16)

    pl.semaphore_wait(barrier, levels + has_ahead.astype(jnp.int32) + has_behind.astype(jnp.int32))

    step = npts // CHUNKS

    def part(chunk):
        return pl.ds((chunk - 1) * step, step)

    def own(kind, chunk, slot, device):
        if chunk == 0:
            return copy((kind, 0), rown, rbuf.at[slot], device)
        return copy((kind, chunk), w.at[part(chunk)], wbuf.at[slot, part(chunk)], device)

    def pass_on(kind, chunk, source, slot, device):
        if chunk == 0:
            return copy((kind, 0), rbuf.at[source], rbuf.at[slot], device)
        return copy((kind, chunk), wbuf.at[source, part(chunk)], wbuf.at[slot, part(chunk)], device)

    def points_copy(level):
        return copy(("pt", level), pbuf.at[level], psib.at[level], partner(level)[0])

    def points_next(level):
        points_copy(level).wait()
        if level + 1 == levels:
            return
        group, width = 1 << level, rank >> level

        def halved(ref):
            return ref[level].reshape(group, width, LANES)[:, : width // 2].reshape(rank // 2, LANES)

        mine, theirs = halved(pbuf), halved(psib)
        upper = partner(level)[1] == 1
        pbuf[level + 1, : rank // 2] = jnp.where(upper, theirs, mine)
        pbuf[level + 1, rank // 2 :] = jnp.where(upper, mine, theirs)
        points_copy(level + 1).start()

    points_copy(0).start()
    for chunk in range(3):
        own("own_x", chunk, 0, xmate).start()

    lw[...] = dot(interp[...], w[...], ((0,), (0,))).astype(BF16)
    half = rank // 2
    kept_at = pl.multiple_of(core * half, half)
    sent_at = pl.multiple_of((1 - core) * half, half)

    def geometry(level, upto):
        bits = reduce_bits(level)
        offset, length = 0, rank
        for bit in bits[:upto]:
            length //= 2
            offset = offset + partner(bit)[1] * length
        if upto:
            offset = pl.multiple_of(offset, length)
        return offset, length

    def reduce_copy(level, at):
        bit = reduce_bits(level)[at]
        length = rank >> (at + 1)
        rows = pl.ds(rank - 2 * length, length)
        return copy(("rs", level, bit), tx.at[level, rows], rx.at[level, rows], partner(bit)[0])

    def exchange_copy(level):
        offset, length = geometry(level, level)
        rows = pl.ds(0 if level == 0 else rank - length, length)
        return copy(("ex", level), tx.at[level, rows], sib.at[level, pl.ds(offset, length)], partner(level)[0])

    def gather_copy(level, at):
        bit = reduce_bits(level)[at]
        offset, length = geometry(level, at + 1)
        rows = pl.ds(offset, length)
        return copy(("ag", level, bit), sib.at[level, rows], sib.at[level, rows], partner(bit)[0])

    for level in range(1, levels):
        tx[level, :half] = dot(trans[level, :, pl.ds(sent_at, half)], lw[...], ((0,), (0,))).astype(BF16)
        reduce_copy(level, 0).start()
        keep[level] = dot(trans[level, :, pl.ds(kept_at, half)], lw[...], ((0,), (0,)))
    tx[0] = dot(trans[0], lw[...], ((0,), (0,))).astype(BF16)
    exchange_copy(0).start()
    for chunk in range(CHUNKS + 1):
        own("own_mate", chunk, 2, mate).start()
    for chunk in range(3, CHUNKS + 1):
        own("own_x", chunk, 0, xmate).start()

    def chain(level):
        bits = reduce_bits(level)
        for at, bit in enumerate(bits):
            reduce_copy(level, at).wait()
            length = rank >> (at + 1)
            total = keep[level, :length] + rx[level, pl.ds(rank - 2 * length, length)].astype(F32)
            if at + 1 < len(bits):
                shorter = length // 2
                upper = partner(bits[at + 1])[1] == 1
                first, second = total[:shorter], total[shorter:]
                tx[level, pl.ds(rank - length, shorter)] = jnp.where(upper, first, second).astype(BF16)
                reduce_copy(level, at + 1).start()
                keep[level, :shorter] = jnp.where(upper, second, first)
            else:
                tx[level, pl.ds(rank - length, length)] = total.astype(BF16)
                exchange_copy(level).start()
            yield
        exchange_copy(level).wait()
        for at in range(len(bits) - 1, -1, -1):
            gather_copy(level, at).start()
            yield
            gather_copy(level, at).wait()

    chains = [chain(level) for level in range(levels)]

    def advance(*which):
        for level in which:
            next(chains[level], None)

    even = chip == 0
    flags = [
        jnp.where(even, mask[0, 3], mask[0, 0]),
        jnp.where(even, mask[0, 0], mask[0, 3]),
        jnp.where(core == 0, mask[0, 2], mask[0, 1]),
        jnp.where(core == 0, mask[0, 1], mask[0, 2]),
    ]
    block = 256

    def near_part(right, weights, flag):
        @pl.loop(0, npts // block)
        def _(at):
            rows = pl.ds(pl.multiple_of(at * block, block), block)
            power = dot(lown[rows, :deep], right[...]) - nown[rows]
            tile = jnp.exp2(power * scale).astype(BF16)
            value = dot(tile, weights[...])
            near[rows] = value if flag is None else near[rows] + flag.astype(F32) * value

    def near_slot(slot):
        near_part(rbuf.at[slot], wbuf.at[slot], flags[slot])

    def couple(level):
        left, norm_own = left_form(pbuf[level].astype(F32), dim)
        power = dot(left, psib[level], ((1,), (1,))) - norm_own
        tile = jnp.exp2(power * scale).astype(BF16)
        coupled = dot(tile, sib[level]).astype(BF16)
        term = dot(trans[level], coupled)
        far[...] = term if level == 0 else far[...] + term

    direct = core == chip

    def relay(chunks):
        for chunk in chunks:
            own("own_x", chunk, 0, xmate).wait_recv()

            @pl.when(has_ahead)
            def _():
                pass_on("fwd", chunk, 0, 1, ahead).start()

            @pl.when(direct)
            def _():
                pass_on("fwd_mate", chunk, 0, 3, mate).start()

    near_part(rown, w, None)
    points_next(0)
    advance(1, 2, 3, 4)
    relay(range(2))
    for chunk in range(CHUNKS + 1):
        own("own_mate", chunk, 2, mate).wait_recv()
    near_slot(2)
    points_next(1)
    advance(1, 2, 3, 4)
    relay(range(2, 3))
    advance(0)
    couple(0)
    points_next(2)
    advance(2, 3, 4, 1)
    relay(range(3, 4))
    couple(1)
    points_next(3)
    advance(2, 3, 4)
    relay(range(4, CHUNKS + 1))
    near_slot(0)
    advance(4, 3, 2)
    points_next(4)
    couple(2)
    advance(4, 3)
    for chunk in range(CHUNKS + 1):
        @pl.when(has_behind)
        def _():
            pass_on("fwd", chunk, 0, 1, ahead).wait_recv()

            @pl.when(jnp.logical_not(direct))
            def _():
                pass_on("fwd_mate", chunk, 1, 3, mate).start()

    advance(4, 3)

    @pl.when(has_behind)
    def _():
        near_slot(1)

    for _ in range(9):
        advance(4, 3)
    couple(3)
    couple(4)

    @pl.when(has_behind | jnp.logical_not(direct))
    def _():
        for chunk in range(CHUNKS + 1):
            pass_on("fwd_mate", chunk, 0, 3, mate).wait_recv()
        near_slot(3)

    total = far[...].astype(BF16)

    @pl.loop(0, npts // block)
    def _(at):
        rows = pl.ds(pl.multiple_of(at * block, block), block)
        out[rows] = (near[rows] + dot(interp[rows], total)).astype(out.dtype)

    for chunk in range(CHUNKS + 1):
        own("own_mate", chunk, 2, mate).wait_send()
        own("own_x", chunk, 0, xmate).wait_send()

        @pl.when(has_ahead)
        def _():
            pass_on("fwd", chunk, 0, 1, ahead).wait_send()

        @pl.when(has_behind | direct)
        def _():
            pass_on("fwd_mate", chunk, 0, 3, mate).wait_send()


def per_device(points, weights, interp, transfers, near_mask, skel_index):
    count = lax.axis_size("leaf")
    dim, npts = points.shape
    rhs, rank = weights.shape[1], interp.shape[1]
    levels = transfers.shape[1]
    deep = -(-(dim + 3) // 16) * 16
    slots = plan(levels)
    vmem = pl.BlockSpec(memory_space=pltpu.VMEM)
    return pl.pallas_call(
        functools.partial(body, count, slots),
        out_shape=jax.ShapeDtypeStruct((npts, rhs), BF16),
        in_specs=[vmem] * 4 + [pl.BlockSpec(memory_space=pltpu.SMEM), vmem],
        out_specs=vmem,
        scratch_shapes=[
            pltpu.VMEM((deep, npts), BF16),
            pltpu.VMEM((npts, LANES), BF16),
            pltpu.VMEM((npts, 1), F32),
            pltpu.VMEM((4, deep, npts), BF16),
            pltpu.VMEM((4, npts, rhs), BF16),
            pltpu.VMEM((npts, rhs), F32),
            pltpu.VMEM((rank, rhs), BF16),
            pltpu.VMEM((levels, rank // 2, rhs), F32),
            pltpu.VMEM((levels, rank, rhs), BF16),
            pltpu.VMEM((levels, rank, rhs), BF16),
            pltpu.VMEM((levels, rank, rhs), BF16),
            pltpu.VMEM((levels, rank, LANES), BF16),
            pltpu.VMEM((levels, rank, LANES), BF16),
            pltpu.VMEM((rank, rhs), F32),
            pltpu.SemaphoreType.DMA((len(slots),)),
            pltpu.SemaphoreType.DMA((len(slots),)),
        ],
        compiler_params=pltpu.CompilerParams(
            collective_id=0, has_side_effects=True, vmem_limit_bytes=60 * 2**20
        ),
    )(points, weights, interp, transfers[0], near_mask, skel_index)


def solution(mesh):
    return jax.shard_map(
        per_device,
        mesh=mesh,
        in_specs=(
            P(None, "leaf"),
            P("leaf", None),
            P("leaf", None),
            P("leaf", None, None, None),
            P("leaf", None),
            P("leaf", None),
        ),
        out_specs=P("leaf", None),
        check_vma=False,
    )
```

time: 256 us -> 91.3 us (0.36)
  the two profiles are of different devices: /device:TPU:0 before, /device:TPU:19 now
where the time goes in v1:
time: 91.3 us; the launch traced here: 91.1 us
  Pallas kernels  88.9 us (97%)
  local copies, waits for them, and re-layouts  2.26 us (2%)
    pallas_call x1, Pallas kernels, per_device(): pl.pallas_call(functools.partial(body, count, slots), out_shape=jax.Shape...  88.9 us
    unnamed x1, local copies, waits for them, and re-layouts  2.26 us

profile of v1, /device:TPU:19, one launch (start us, length us, event | category | flops | bytes accessed | tf_op | source)
XLA Modules:
  0.0 91.1 jit_solution(15498560759614579158)
XLA Ops:
  0.0 88.9 %shard_map.64 = bf16[1024,512]{1,0:T(8,128)(2,1)} custom-call(bf16[64,1024]{1,0:T(8,128)(2,1)} %pts.1, bf16[1024,512]{1,0:T(8,128)(2,1)} %w.1, bf16[1024,512]{1,0:T(8,128)(2,1)} %interp.1, bf16[5,512,512]{2,1,0:T(8,128)(2,1)} %bitcast.1, s32[1,4]{1,0:T(1,128)} %mask.1, s32[1,512]{1,0:T(1,128)} %index.1), custom_call_target="tpu_custom_call" | custom-call | tf_op jit(solution)/shard_map/pallas_call | solution.py:334
  88.9 2.3 %copy.8 = bf16[1024,512]{1,0:T(8,128)(2,1)} copy(bf16[1024,512]{1,0:T(8,128)(2,1)} %shard_map.64) | data formatting | bytes 2097152

commit v2 on v1

--- a/solution.py
+++ b/solution.py
@@ -10,7 +10,7 @@
 
 MESH = pl.DeviceIdType.MESH
 LANES = 128
-CHUNKS = 4
+CHUNKS = 8
 F32, BF16 = jnp.float32, jnp.bfloat16
 
 
@@ -135,10 +135,16 @@
         points_copy(level + 1).start()
 
     points_copy(0).start()
-    for chunk in range(3):
-        own("own_x", chunk, 0, xmate).start()
+
+    def send_x(*chunks):
+        for chunk in chunks:
+            own("own_x", chunk, 0, xmate).start()
+
+    send_x(0, 1)
 
     lw[...] = dot(interp[...], w[...], ((0,), (0,))).astype(BF16)
+    points_next(0)
+    send_x(2)
     half = rank // 2
     kept_at = pl.multiple_of(core * half, half)
     sent_at = pl.multiple_of((1 - core) * half, half)
@@ -170,7 +176,7 @@
         rows = pl.ds(offset, length)
         return copy(("ag", level, bit), sib.at[level, rows], sib.at[level, rows], partner(bit)[0])
 
-    for level in range(1, levels):
+    for level in range(levels - 1, 0, -1):
         tx[level, :half] = dot(trans[level, :, pl.ds(sent_at, half)], lw[...], ((0,), (0,))).astype(BF16)
         reduce_copy(level, 0).start()
         keep[level] = dot(trans[level, :, pl.ds(kept_at, half)], lw[...], ((0,), (0,)))
@@ -178,8 +184,6 @@
     exchange_copy(0).start()
     for chunk in range(CHUNKS + 1):
         own("own_mate", chunk, 2, mate).start()
-    for chunk in range(3, CHUNKS + 1):
-        own("own_x", chunk, 0, xmate).start()
 
     def chain(level):
         bits = reduce_bits(level)
@@ -219,8 +223,8 @@
     ]
     block = 256
 
-    def near_part(right, weights, flag):
-        @pl.loop(0, npts // block)
+    def near_part(right, weights, flag, first=0, last=npts // block):
+        @pl.loop(first, last)
         def _(at):
             rows = pl.ds(pl.multiple_of(at * block, block), block)
             power = dot(lown[rows, :deep], right[...]) - nown[rows]
@@ -241,7 +245,7 @@
 
     direct = core == chip
 
-    def relay(chunks):
+    def relay(*chunks):
         for chunk in chunks:
             own("own_x", chunk, 0, xmate).wait_recv()
 
@@ -253,49 +257,76 @@
             def _():
                 pass_on("fwd_mate", chunk, 0, 3, mate).start()
 
-    near_part(rown, w, None)
-    points_next(0)
-    advance(1, 2, 3, 4)
-    relay(range(2))
+    def relay_on(*chunks):
+        for chunk in chunks:
+            @pl.when(has_behind)
+            def _():
+                pass_on("fwd", chunk, 0, 1, ahead).wait_recv()
+
+                @pl.when(jnp.logical_not(direct))
+                def _():
+                    pass_on("fwd_mate", chunk, 1, 3, mate).start()
+
+    tiles = npts // block
+    advance(4, 3, 2, 1)
+    send_x(3)
+    near_part(rown, w, None, 0, tiles // 2)
+    relay(0, 1)
+    points_next(1)
+
+    advance(4, 3, 2)
+    send_x(4)
+    near_part(rown, w, None, tiles // 2, tiles)
+    relay(2)
+    points_next(2)
+
+    advance(4, 3, 2)
+    send_x(5)
     for chunk in range(CHUNKS + 1):
         own("own_mate", chunk, 2, mate).wait_recv()
     near_slot(2)
-    points_next(1)
-    advance(1, 2, 3, 4)
-    relay(range(2, 3))
-    advance(0)
+    relay(3)
+    relay_on(0, 1)
+    points_next(3)
+
+    advance(4, 3, 2)
+    send_x(6)
+    advance(1, 0)
     couple(0)
-    points_next(2)
-    advance(2, 3, 4, 1)
-    relay(range(3, 4))
+    relay(4)
+    relay_on(2)
+    points_next(4)
+
+    advance(4, 3, 2)
+    send_x(7)
+    advance(1)
     couple(1)
-    points_next(3)
-    advance(2, 3, 4)
-    relay(range(4, CHUNKS + 1))
+    relay(5)
+    relay_on(3)
+
+    advance(4, 3)
+    send_x(8)
+    couple(2)
+    relay(6)
+    relay_on(4)
+
+    advance(4, 3)
+    couple(3)
+    relay(7)
+    relay_on(5)
+
+    advance(4)
+    relay(8)
     near_slot(0)
-    advance(4, 3, 2)
-    points_next(4)
-    couple(2)
-    advance(4, 3)
-    for chunk in range(CHUNKS + 1):
-        @pl.when(has_behind)
-        def _():
-            pass_on("fwd", chunk, 0, 1, ahead).wait_recv()
-
-            @pl.when(jnp.logical_not(direct))
-            def _():
-                pass_on("fwd_mate", chunk, 1, 3, mate).start()
-
-    advance(4, 3)
+    relay_on(6)
+
+    advance(4)
+    couple(4)
+    relay_on(7, 8)
 
     @pl.when(has_behind)
     def _():
         near_slot(1)
-
-    for _ in range(9):
-        advance(4, 3)
-    couple(3)
-    couple(4)
 
     @pl.when(has_behind | jnp.logical_not(direct))
     def _():

time: 91.3 us -> 75.6 us (0.83)
  the two profiles are of different devices: /device:TPU:19 before, /device:TPU:12 now
where the time goes in v2:
time: 75.6 us; the launch traced here: 75.4 us
  Pallas kernels  73.1 us (97%)
  local copies, waits for them, and re-layouts  2.26 us (3%)
    pallas_call x1, Pallas kernels, per_device(): pl.pallas_call(functools.partial(body, count, slots), out_shape=jax.Shape...  73.1 us
    unnamed x1, local copies, waits for them, and re-layouts  2.26 us

profile of v2, /device:TPU:12, one launch (start us, length us, event | category | flops | bytes accessed | tf_op | source)
XLA Modules:
  0.0 75.4 jit_solution(18004400787106119403)
XLA Ops:
  0.0 73.1 %shard_map.64 = bf16[1024,512]{1,0:T(8,128)(2,1)} custom-call(bf16[64,1024]{1,0:T(8,128)(2,1)} %pts.1, bf16[1024,512]{1,0:T(8,128)(2,1)} %w.1, bf16[1024,512]{1,0:T(8,128)(2,1)} %interp.1, bf16[5,512,512]{2,1,0:T(8,128)(2,1)} %bitcast.1, s32[1,4]{1,0:T(1,128)} %mask.1, s32[1,512]{1,0:T(1,128)} %index.1), custom_call_target="tpu_custom_call" | custom-call | tf_op jit(solution)/shard_map/pallas_call | solution.py:365
  73.2 2.3 %copy.8 = bf16[1024,512]{1,0:T(8,128)(2,1)} copy(bf16[1024,512]{1,0:T(8,128)(2,1)} %shard_map.64) | data formatting | bytes 2097152
